TPU v7x, 128 devices: a whole 4x4x4 slice. The times are simulated.
128 devices in a mesh: row: 16 (over y, x), col: 8 (over z, core).
Axes of the slice: x: 4, y: 4, z: 4, core: 2. Of those that a mesh axis runs over, the one named last changes fastest.
Arguments:
- features: bfloat16 [32768, 256], P(('row', 'col')), may hold values from -6 to 6
- out_degree: int32 [32768], P('row'), may hold values from 8 to 1024
- in_degree: int32 [32768], P('col'), may hold values from 8 to 1024
- tile_blocks: int32 [16, 8, 2, 128], P('row', 'col'), may hold values from 0 to 31, as said below
- tile_count: int32 [16, 8], P('row', 'col'), may hold values from 16 to 128, as said below
- tile_weights: bfloat16 [16, 8, 128, 128, 128], P('row', 'col'), may hold values from 0 to 4, as said below
- weight: bfloat16 [256, 256], replicated, may hold values from -0.375 to 0.375
- cotangent: bfloat16 [32768, 256], P(('col', 'row')), may hold values from -6 to 6
Outputs:
- hidden: bfloat16 [32768, 256], P(('col', 'row'))
- input_grad: bfloat16 [32768, 256], P(('row', 'col'))
- weight_grad: float32 [256, 256], replicated
Inputs may be any that keep to these rules, and one draw needn't show every extreme that they name: `tile_blocks`: entry [r, c, 0, s] is a target block below 32, entry [r, c, 1, s] a source block below 16; the pairs of one device position are distinct. `tile_count`: live tile slots of a device position are its first ones; some position has exactly 128. `tile_weights`: Non-negative edge weights.
All inputs are finite; a program needn't handle non-finite values.
Results may differ from a plain program's by a relative error of at most 0.0067.
Values may be sent and summed in bfloat16 or wider, within the bound.
No kernel may reach another device: no remote copies, remote signals or barrier semaphores. Data moves between devices by JAX's collectives and lax.ppermute only.
A program may use at most 192 MiB of HBM per device.

v0:
```python
import jax
import jax.numpy as jnp
from jax import lax
from jax.sharding import PartitionSpec as P

TILE = 128


def silu_slope(pre_act):
    gate_sig = jax.nn.sigmoid(pre_act)
    return gate_sig * (1.0 + pre_act * (1.0 - gate_sig))


def tile_sum(tile_vals, dst_ids, src_ids, live_count, inputs, dst_blocks, transpose):
    feat_width = inputs.shape[1]
    group_size = min(128, tile_vals.shape[0])
    block_stack = inputs.reshape(-1, TILE, feat_width)
    group_count = (live_count + group_size - 1) // group_size

    def add_group(group_at, running):
        first_slot = group_at * group_size
        picked = jnp.take(block_stack, src_ids, axis=0)
        if transpose:
            products = jnp.einsum(
                "trc,trh->tch", tile_vals, picked, preferred_element_type=jnp.float32
            )
        else:
            products = jnp.einsum(
                "trc,tch->trh", tile_vals, picked, preferred_element_type=jnp.float32
            )
        slot_ids = first_slot + jnp.arange(group_size)
        is_live = slot_ids < live_count
        masked = jnp.where(is_live[:, None], products.reshape(group_size, -1), 0.0)
        return running.at[dst_ids].add(masked)

    start_sum = jnp.zeros((dst_blocks, TILE * feat_width), jnp.float32)
    running = lax.fori_loop(0, group_count, add_group, start_sum)
    return running.reshape(dst_blocks * TILE, feat_width)


def shards(
    features, out_degree, in_degree, tile_blocks, tile_count, tile_weights, weight, cotangent
):
    row_count = features.shape[0]
    row_at = lax.axis_index("row")
    col_at = lax.axis_index("col")
    out_strip = lax.rsqrt(out_degree.astype(jnp.float32))
    in_strip = lax.rsqrt(in_degree.astype(jnp.float32))
    own_out = lax.dynamic_slice_in_dim(out_strip, col_at * row_count, row_count, 0)
    src_scaled = (features.astype(jnp.float32) * own_out[:, None]).astype(jnp.bfloat16)
    source = lax.all_gather(src_scaled, "col", axis=0, tiled=True)
    blocks = tile_blocks[0, 0]
    live_count = tile_count[0, 0]
    tile_vals = tile_weights[0, 0]
    partial_value = tile_sum(
        tile_vals, blocks[0], blocks[1], live_count, source, in_strip.shape[0] // TILE, False
    )
    contract_rows = (((0,), (0,)), ((), ()))
    summed = lax.psum(partial_value, "row")
    agg_strip = (summed * in_strip[:, None]).astype(jnp.bfloat16)
    pre_strip = jnp.dot(agg_strip, weight, preferred_element_type=jnp.float32)
    strip_grads = lax.all_gather(cotangent, "row", axis=0, tiled=True)
    grad_strip = (strip_grads.astype(jnp.float32) * silu_slope(pre_strip)).astype(jnp.bfloat16)
    own_pre = lax.dynamic_slice_in_dim(pre_strip, row_at * row_count, row_count, 0)
    hidden = jax.nn.silu(own_pre).astype(jnp.bfloat16)
    agg_rows = lax.dynamic_slice_in_dim(agg_strip, row_at * row_count, row_count, 0)
    pre_grad = lax.dynamic_slice_in_dim(grad_strip, row_at * row_count, row_count, 0)
    weight_part = lax.dot_general(
        agg_rows, pre_grad, contract_rows, preferred_element_type=jnp.float32
    )
    back_rows = jnp.dot(grad_strip, weight.T, preferred_element_type=jnp.float32)
    target_grad = (back_rows * in_strip[:, None]).astype(jnp.bfloat16)
    weight_grad = lax.psum(weight_part, ("row", "col"))
    back_part = tile_sum(
        tile_vals, blocks[1], blocks[0], live_count, target_grad, source.shape[0] // TILE, True
    )
    src_sum = lax.psum_scatter(back_part, "col", scatter_dimension=0, tiled=True)
    input_grad = (src_sum * own_out[:, None]).astype(jnp.bfloat16)
    return (hidden, input_grad, weight_grad)


def solution(mesh):
    placed = (
        P(("row", "col"), None),
        P("row"),
        P("col"),
        P("row", "col", None, None),
        P("row", "col"),
        P("row", "col", None, None, None),
        P(),
        P(("col", "row"), None),
    )
    return jax.shard_map(
        shards,
        mesh=mesh,
        in_specs=placed,
        out_specs=(P(("col", "row"), None), P(("row", "col"), None), P()),
        check_vma=False,
    )
```

profile of v0, /device:TPU:1, one launch (start us, length us, event | category | flops | bytes accessed | tf_op | source)
XLA Modules:
  0.0 580.1 jit_solution(587805703968408114)
XLA Ops:
  7.2 0.0 copy-start
  7.2 0.0 all-gather.3.cloned.1.call-start
  7.2 0.8 fusion.16
  8.0 0.0 copy-start.6
  8.0 0.5 copy-done.6
  8.5 1.7 multiply_convert_fusion.4
  10.2 0.0 all-gather.3.cloned.1.call-update
  10.2 0.0 all-reduce.3.cloned.1.call-start
  10.9 0.8 slice_bitcast_fusion
  11.7 25.7 %all-gather.3.cloned.1.call-done = bf16[2048,256]{1,0:T(8,128)(2,1)} async-done(((bf16[256,256]{1,0:T(8,128)(2,1)}), bf16[2048,256]{1,0:T(8,128)(2,1)}) %all-gather.3.cloned.1.call-update) | async-done | bytes 1048592 | tf_op jit(solution)/shard_map/all_gather | solution.py:51
  37.4 0.0 copy-start.2
  37.4 2.3 broadcast_in_dim.54
  39.7 0.0 copy-done.2
  39.7 94.9 %while.20 = (s32[]{:T(128)}, f32[32,32768]{1,0:T(8,128)}, s32[]{:T(128)}, s32[128]{0:T(128)S(1)}, s32[]{:T(128)}, /*index=5*/s32[128]{0:T(128)S(1)}, bf16[16,128...) while((s32[]{:T(128)}, f32[32,32768]{1,0:T(8,128)}, s32[]{:T(128)}, ...), condition=%wide.region_2.3_spmd, body=%wide.region_0.2_spmd.sunk | while | flops 1086327552 | bytes 197141120 | solution.py:37
  39.8 6.6 %gather_fusion = bf16[128,128,256]{2,1,0:T(8,128)(2,1)} fusion(bf16[16,128,256]{2,1,0:T(8,128)(2,1)S(1)} %get-tuple-element.277, s32[1024]{0:T(1024)S(1)} %pad_clamp_fusion.4), kind=kCustom, calls=%fused_computation.clone.1 | custom fusion | bytes 16777728 | tf_op jit(solution)/shard_map/while/body/jit(_take)/gather | solution.py:22
  46.3 0.7 compare_and_fusion.4
  47.0 13.2 %convolution_bitcast_fusion.4 = f32[128,128,256]{1,2,0:T(8,128)} fusion(bf16[128,128,128]{2,1,0:T(8,128)(2,1)} %get-tuple-element.278, bf16[128,128,256]{2,1,0:T(8,128)(2,1)} %gather_fusion, pred[128]{0:T(512)(128)(4,1)S(1)} %get-tuple-element.237), kind=kOutput, calls=%fused_computation.5.clone.1 | convolution fusion | flops 1077936128 | bytes 29360256 | tf_op jit(solution)/shard_map/while/body/trc,tch->trh/dot_general | solution.py:28
  60.2 17.7 %copy.29 = f32[128,128,256]{0,2,1:T(8,128)} copy(f32[128,128,256]{1,2,0:T(8,128)} %convolution_bitcast_fusion.4) | data formatting | bytes 33554432 | tf_op jit(solution)/shard_map/while/body/trc,tch->trh/dot_general | solution.py:28
  77.9 11.2 %bitcast_select_fusion.4 = f32[128,32768]{0,1:T(8,128)} fusion(f32[128,128,256]{0,2,1:T(8,128)} %copy.29, pred[128]{0:T(512)(128)(4,1)S(1)} %get-tuple-element.238), kind=kLoop, calls=%fused_computation.4.clone.1 | loop fusion | flops 4194304 | bytes 33554560 | tf_op jit(solution)/shard_map/while/body/jit(_where)/select_n | solution.py:33
  89.1 17.4 %copy.30 = f32[128,32768]{1,0:T(8,128)} copy(f32[128,32768]{0,1:T(8,128)} %bitcast_select_fusion.4) | data formatting | bytes 33554432 | tf_op jit(solution)/shard_map/while/body/jit(_where)/select_n | solution.py:33
  106.6 27.7 %scatter_fusion = f32[32,32768]{1,0:T(8,128)} fusion(f32[32,32768]{1,0:T(8,128)} %get-tuple-element.262, s32[128]{0:T(128)S(1)} %get-tuple-element.235, f32[128,32768]{1,0:T(8,128)} %copy.30), kind=kCustom, calls=%fused_computation.2.clone.1 | custom fusion | flops 4194304 | bytes 50332160 | tf_op jit(solution)/shard_map/while/body/scatter-add | solution.py:34
  134.6 4.9 reshape.111
  139.5 0.0 copy-start.5
  139.5 0.0 all-reduce.3.cloned.1.call-update
  139.5 0.0 all-gather.5.cloned.1.call-start
  139.6 0.7 all-gather.5.cloned.1.call-update
  140.3 0.0 reduce-scatter.2.cloned.1.call-start
  140.3 0.0 copy-done.5
  140.4 101.8 %all-reduce.3.cloned.1.call-done = f32[4096,256]{1,0:T(8,128)} async-done(((f32[4096,256]{1,0:T(8,128)}), f32[4096,256]{1,0:T(8,128)}) %all-reduce.3.cloned.1.call-update) | async-done | bytes 4194320 | tf_op jit(solution)/shard_map/psum | solution.py:59
  242.2 2.6 multiply_convert_fusion.1
  244.7 0.0 copy-start.3
  244.7 42.9 %all-gather.5.cloned.1.call-done = bf16[4096,256]{1,0:T(8,128)(2,1)} async-done(((bf16[256,256]{1,0:T(8,128)(2,1)}), bf16[4096,256]{1,0:T(8,128)(2,1)}) %all-gather.5.cloned.1.call-update) | async-done | bytes 2097168 | tf_op jit(solution)/shard_map/all_gather | solution.py:62
  287.6 0.0 copy-done
  287.7 5.2 multiply_convert_fusion
  292.9 0.0 copy-done.3
  292.9 0.0 copy-start.4
  292.9 2.0 fusion.12
  294.9 0.0 copy-done.4
  294.9 0.1 broadcast_in_dim.55
  295.0 92.8 %while.21 = (s32[]{:T(128)}, f32[16,32768]{1,0:T(8,128)S(1)}, s32[]{:T(128)}, s32[128]{0:T(128)S(1)}, s32[]{:T(128)}, /*index=5*/s32[128]{0:T(128)S(1)}, bf16[32...) while((s32[]{:T(128)}, f32[16,32768]{1,0:T(8,128)S(1)}, s32[]{:T(128)}, ...), condition=%wide.region_6.7_spmd, body=%wide.region_4.6_spmd.sunk | while | flops 1086327552 | bytes 197141120 | solution.py:37
  295.3 8.2 %gather_fusion.1 = bf16[128,128,256]{2,1,0:T(8,128)(2,1)} fusion(bf16[32,128,256]{2,1,0:T(8,128)(2,1)} %get-tuple-element.307, s32[1024]{0:T(1024)S(1)} %pad_clamp_fusion.5), kind=kCustom, calls=%fused_computation.1.clone.1 | custom fusion | bytes 16777728 | tf_op jit(solution)/shard_map/while/body/jit(_take)/gather | solution.py:22
  303.4 0.7 compare_and_fusion.5
  304.1 12.8 %convolution_bitcast_fusion.5 = f32[128,128,256]{1,2,0:T(8,128)} fusion(bf16[128,128,128]{2,1,0:T(8,128)(2,1)} %get-tuple-element.308, bf16[128,128,256]{2,1,0:T(8,128)(2,1)} %gather_fusion.1, pred[128]{0:T(512)(128)(4,1)S(1)} %get-tuple-element.249), kind=kOutput, calls=%fused_computation.19.clone.1 | convolution fusion | flops 1077936128 | bytes 29360256 | tf_op jit(solution)/shard_map/while/body/trc,trh->tch/dot_general | solution.py:24
  316.9 17.7 %copy.31 = f32[128,128,256]{0,2,1:T(8,128)} copy(f32[128,128,256]{1,2,0:T(8,128)} %convolution_bitcast_fusion.5) | data formatting | bytes 33554432 | tf_op jit(solution)/shard_map/while/body/trc,trh->tch/dot_general | solution.py:24
  334.6 11.3 %bitcast_select_fusion.5 = f32[128,32768]{0,1:T(8,128)} fusion(f32[128,128,256]{0,2,1:T(8,128)} %copy.31, pred[128]{0:T(512)(128)(4,1)S(1)} %get-tuple-element.250), kind=kLoop, calls=%fused_computation.18.clone.1 | loop fusion | flops 4194304 | bytes 33554560 | tf_op jit(solution)/shard_map/while/body/jit(_where)/select_n | solution.py:33
  345.9 17.4 %copy.32 = f32[128,32768]{1,0:T(8,128)} copy(f32[128,32768]{0,1:T(8,128)} %bitcast_select_fusion.5) | data formatting | bytes 33554432 | tf_op jit(solution)/shard_map/while/body/jit(_where)/select_n | solution.py:33
  363.3 24.3 %scatter_fusion.1 = f32[16,32768]{1,0:T(8,128)S(1)} fusion(f32[16,32768]{1,0:T(8,128)S(1)} %get-tuple-element.292, s32[128]{0:T(128)S(1)} %get-tuple-element.247, f32[128,32768]{1,0:T(8,128)} %copy.32), kind=kCustom, calls=%fused_computation.3.clone.1 | custom fusion | flops 4194304 | bytes 50332160 | tf_op jit(solution)/shard_map/while/body/scatter-add | solution.py:34
  387.9 0.0 copy-start.7
  387.9 0.0 copy-start.1
  387.9 1.5 reshape.113
  389.4 0.0 reduce-scatter.2.cloned.1.call-update
  389.4 0.0 all-reduce.5.cloned.1.call-start
  389.5 1.7 multiply_convert_fusion.3
  391.2 1.9 fusion.13
  393.1 0.0 all-reduce.5.cloned.1.call-update
  393.1 28.5 %reduce-scatter.2.cloned.1.call-done = f32[256,256]{1,0:T(8,128)} async-done(((f32[2048,256]{1,0:T(8,128)}), f32[256,256]{1,0:T(8,128)}) %reduce-scatter.2.cloned.1.call-update) | async-done | bytes 262160 | tf_op jit(solution)/shard_map/reduce_scatter | solution.py:77
  421.5 0.0 copy-done.7
  421.5 1.7 multiply_convert_fusion.2
  423.3 148.3 %all-reduce.5.cloned.1.call-done = f32[256,256]{1,0:T(8,128)} async-done(((f32[256,256]{1,0:T(8,128)}), f32[256,256]{1,0:T(8,128)}) %all-reduce.5.cloned.1.call-update) | async-done | bytes 262160 | tf_op jit(solution)/shard_map/psum | solution.py:73
  571.6 1.7 copy.50
  573.3 0.0 copy-done.1
  (5 shorter events, 0.0 us)
Async XLA Ops:
  7.2 280.5 %copy-start = (bf16[256,256]{1,0:T(8,128)(2,1)S(1)}, bf16[256,256]{1,0:T(8,128)(2,1)}, u32[]{:S(2)}) copy-start(bf16[256,256]{1,0:T(8,128)(2,1)} %param.18) | copy-start | bytes 393220
  7.2 30.2 %all-gather.3.cloned.1.call-start = ((), (), s32[]{:S(2)}) async-start(), calls=%async_computation.1 | async-start | bytes 1179648 | tf_op jit(solution)/shard_map/all_gather | solution.py:51
  8.0 0.5 copy-start.6
  10.2 231.9 %all-reduce.3.cloned.1.call-start = ((), (), s32[]{:S(2)}) async-start(), calls=%async_computation.2 | async-start | bytes 8388608 | tf_op jit(solution)/shard_map/psum | solution.py:59
  37.4 2.3 copy-start.2
  139.5 0.8 copy-start.5
  139.5 148.1 %all-gather.5.cloned.1.call-start = ((), (), s32[]{:S(2)}) async-start(), calls=%async_computation.3 | async-start | bytes 2228224 | tf_op jit(solution)/shard_map/all_gather | solution.py:62
  140.3 281.3 %reduce-scatter.2.cloned.1.call-start = ((), (), s32[]{:S(2)}) async-start(), calls=%async_computation.4 | async-start | bytes 2359296 | tf_op jit(solution)/shard_map/reduce_scatter | solution.py:77
  244.7 48.1 %copy-start.3 = (bf16[4096,256]{1,0:T(8,128)(2,1)}, bf16[4096,256]{1,0:T(8,128)(2,1)S(1)}, u32[]{:S(2)}) copy-start(bf16[4096,256]{1,0:T(8,128)(2,1)S(1)} %multiply_convert_fusion.1) | copy-start | bytes 6291460
  292.9 2.0 copy-start.4
  387.9 33.7 %copy-start.7 = (f32[256]{0:T(256)S(1)}, f32[256]{0:T(256)}, u32[]{:S(2)}) copy-start(f32[256]{0:T(256)} %copy-done.6) | copy-start | bytes 3076
  387.9 185.4 %copy-start.1 = (bf16[256,256]{1,0:T(8,128)(2,1)S(1)}, bf16[256,256]{1,0:T(8,128)(2,1)}, u32[]{:S(2)}) copy-start(bf16[256,256]{1,0:T(8,128)(2,1)} %param.18) | copy-start | bytes 393220
  389.4 182.2 %all-reduce.5.cloned.1.call-start = ((), (), s32[]{:S(2)}) async-start(), calls=%async_computation.5 | async-start | bytes 524288 | tf_op jit(solution)/shard_map/psum | solution.py:73
Sparse Core Ops, SparseCore 0:
  10.3 27.0 all-gather.2
  139.7 102.4 all-reduce.2
  244.3 43.3 all-gather.4
  389.5 31.9 reduce-scatter.1
  426.7 144.8 all-reduce.4
where the time goes:
time: 582 us; the launch traced here: 580 us
  waiting for transfers between devices  348 us (60%)
  local copies, waits for them, and re-layouts  96.8 us (17%)
  other arithmetic  84.3 us (14%)
  matrix products  35.2 us (6%)
  between operations  14.8 us (3%)
    psum x1, waiting for transfers between devices, shards(): weight_grad = lax.psum(weight_part, ('row', 'col'))  148 us
    psum x1, waiting for transfers between devices, shards(): summed = lax.psum(partial_value, 'row')  102 us
    scatter-add x2, other arithmetic, add_group(): return running.at[dst_ids].add(masked)  52 us
    all_gather x1, waiting for transfers between devices, shards(): strip_grads = lax.all_gather(cotangent, 'row', axis=0, tiled=True)  42.9 us
    select_n x2, local copies, waits for them, and re-layouts, add_group(): masked = jnp.where(is_live[:, None], products.reshape(group_size, -1), 0.0)  34.9 us
    reduce_scatter x1, waiting for transfers between devices, shards(): lax.psum_scatter(back_part, 'col', scatter_dimension=0, tiled=True)  28.5 us
    all_gather x1, waiting for transfers between devices, shards(): source = lax.all_gather(src_scaled, 'col', axis=0, tiled=True)  25.7 us
    select_n x2, other arithmetic, add_group(): masked = jnp.where(is_live[:, None], products.reshape(group_size, -1), 0.0)  22.5 us
  transfers between devices with their start and end apart: 5, of which 5 were waited for; matrix products, arithmetic and copies ran while one was open for 1% of the time, Pallas kernels for 0%

commit v1 on v0

--- a/solution.py
+++ b/solution.py
@@ -70,7 +70,7 @@
     )
     back_rows = jnp.dot(grad_strip, weight.T, preferred_element_type=jnp.float32)
     target_grad = (back_rows * in_strip[:, None]).astype(jnp.bfloat16)
-    weight_grad = lax.psum(weight_part, ("row", "col"))
+    weight_grad = lax.psum(lax.psum(weight_part, "col"), "row")
     back_part = tile_sum(
         tile_vals, blocks[1], blocks[0], live_count, target_grad, source.shape[0] // TILE, True
     )

time: 582 us -> 522 us (0.90)
  waiting for transfers between devices: 348 us -> 287 us
    psum x1 -> x2, waiting for transfers between devices: 148 us -> 85.8 us  [shards(): weight_grad = lax.psum(lax.psum(weight_part, 'col'), 'row')]
  transfers between devices with their start and end apart: 5 -> 6, of which waited for: 5 -> 5; matrix products, arithmetic and copies ran while one was open for 1% -> 19% of each run, Pallas kernels for 0% -> 0%
where the time goes in v1:
time: 522 us; the launch traced here: 519 us
  waiting for transfers between devices  287 us (55%)
  local copies, waits for them, and re-layouts  96.8 us (19%)
  other arithmetic  84.3 us (16%)
  matrix products  34.2 us (7%)
  between operations  15.2 us (3%)
    psum x1, waiting for transfers between devices, shards(): summed = lax.psum(partial_value, 'row')  102 us
    psum x2, waiting for transfers between devices, shards(): weight_grad = lax.psum(lax.psum(weight_part, 'col'), 'row')  85.8 us
    scatter-add x2, other arithmetic, add_group(): return running.at[dst_ids].add(masked)  52 us
    all_gather x1, waiting for transfers between devices, shards(): strip_grads = lax.all_gather(cotangent, 'row', axis=0, tiled=True)  42.9 us
    select_n x2, local copies, waits for them, and re-layouts, add_group(): masked = jnp.where(is_live[:, None], products.reshape(group_size, -1), 0.0)  34.9 us
    reduce_scatter x1, waiting for transfers between devices, shards(): lax.psum_scatter(back_part, 'col', scatter_dimension=0, tiled=True)  29.9 us
    all_gather x1, waiting for transfers between devices, shards(): source = lax.all_gather(src_scaled, 'col', axis=0, tiled=True)  25.7 us
    select_n x2, other arithmetic, add_group(): masked = jnp.where(is_live[:, None], products.reshape(group_size, -1), 0.0)  22.6 us
  transfers between devices with their start and end apart: 6, of which 5 were waited for; matrix products, arithmetic and copies ran while one was open for 19% of the time, Pallas kernels for 0%

profile of v1, /device:TPU:1, one launch (start us, length us, event | category | flops | bytes accessed | tf_op | source)
XLA Modules:
  0.0 518.8 jit_solution(11398628376541662829)
XLA Ops:
  7.2 0.0 copy-start
  7.2 0.0 all-gather.3.cloned.1.call-start
  7.2 0.8 fusion.16
  8.0 0.0 copy-start.4
  8.0 0.6 copy-done.4
  8.6 1.7 multiply_convert_fusion.4
  10.3 0.0 all-gather.3.cloned.1.call-update
  10.3 0.0 all-reduce.4.cloned.1.call-start
  11.0 0.8 slice_bitcast_fusion
  11.8 25.7 %all-gather.3.cloned.1.call-done = bf16[2048,256]{1,0:T(8,128)(2,1)} async-done(((bf16[256,256]{1,0:T(8,128)(2,1)}), bf16[2048,256]{1,0:T(8,128)(2,1)}) %all-gather.3.cloned.1.call-update) | async-done | bytes 1048592 | tf_op jit(solution)/shard_map/all_gather | solution.py:51
  37.5 0.0 copy-start.2
  37.5 2.3 broadcast_in_dim.54
  39.8 0.0 copy-done.2
  39.8 94.8 %while.20 = (s32[]{:T(128)}, f32[32,32768]{1,0:T(8,128)}, s32[]{:T(128)}, s32[128]{0:T(128)S(1)}, s32[]{:T(128)}, /*index=5*/s32[128]{0:T(128)S(1)}, bf16[16,128...) while((s32[]{:T(128)}, f32[32,32768]{1,0:T(8,128)}, s32[]{:T(128)}, ...), condition=%wide.region_2.3_spmd, body=%wide.region_0.2_spmd.sunk | while | flops 1086327552 | bytes 197141120 | solution.py:37
  39.8 6.6 %gather_fusion = bf16[128,128,256]{2,1,0:T(8,128)(2,1)} fusion(bf16[16,128,256]{2,1,0:T(8,128)(2,1)S(1)} %get-tuple-element.277, s32[1024]{0:T(1024)S(1)} %pad_clamp_fusion.4), kind=kCustom, calls=%fused_computation.clone.1 | custom fusion | bytes 16777728 | tf_op jit(solution)/shard_map/while/body/jit(_take)/gather | solution.py:22
  46.4 0.7 compare_and_fusion.4
  47.1 13.2 %convolution_bitcast_fusion.4 = f32[128,128,256]{1,2,0:T(8,128)} fusion(bf16[128,128,128]{2,1,0:T(8,128)(2,1)} %get-tuple-element.278, bf16[128,128,256]{2,1,0:T(8,128)(2,1)} %gather_fusion, pred[128]{0:T(512)(128)(4,1)S(1)} %get-tuple-element.237), kind=kOutput, calls=%fused_computation.5.clone.1 | convolution fusion | flops 1077936128 | bytes 29360256 | tf_op jit(solution)/shard_map/while/body/trc,tch->trh/dot_general | solution.py:28
  60.3 17.6 %copy.29 = f32[128,128,256]{0,2,1:T(8,128)} copy(f32[128,128,256]{1,2,0:T(8,128)} %convolution_bitcast_fusion.4) | data formatting | bytes 33554432 | tf_op jit(solution)/shard_map/while/body/trc,tch->trh/dot_general | solution.py:28
  77.9 11.2 %bitcast_select_fusion.4 = f32[128,32768]{0,1:T(8,128)} fusion(f32[128,128,256]{0,2,1:T(8,128)} %copy.29, pred[128]{0:T(512)(128)(4,1)S(1)} %get-tuple-element.238), kind=kLoop, calls=%fused_computation.4.clone.1 | loop fusion | flops 4194304 | bytes 33554560 | tf_op jit(solution)/shard_map/while/body/jit(_where)/select_n | solution.py:33
  89.1 17.4 %copy.30 = f32[128,32768]{1,0:T(8,128)} copy(f32[128,32768]{0,1:T(8,128)} %bitcast_select_fusion.4) | data formatting | bytes 33554432 | tf_op jit(solution)/shard_map/while/body/jit(_where)/select_n | solution.py:33
  106.6 27.7 %scatter_fusion = f32[32,32768]{1,0:T(8,128)} fusion(f32[32,32768]{1,0:T(8,128)} %get-tuple-element.262, s32[128]{0:T(128)S(1)} %get-tuple-element.235, f32[128,32768]{1,0:T(8,128)} %copy.30), kind=kCustom, calls=%fused_computation.2.clone.1 | custom fusion | flops 4194304 | bytes 50332160 | tf_op jit(solution)/shard_map/while/body/scatter-add | solution.py:34
  134.6 4.9 reshape.111
  139.5 0.0 copy-start.3
  139.5 0.0 all-reduce.4.cloned.1.call-update
  139.5 0.0 all-gather.5.cloned.1.call-start
  139.6 0.7 all-gather.5.cloned.1.call-update
  140.3 0.0 all-reduce.6.cloned.1.call-start
  140.3 0.0 copy-done.3
  140.3 101.8 %all-reduce.4.cloned.1.call-done = f32[4096,256]{1,0:T(8,128)} async-done(((f32[4096,256]{1,0:T(8,128)}), f32[4096,256]{1,0:T(8,128)}) %all-reduce.4.cloned.1.call-update) | async-done | bytes 4194320 | tf_op jit(solution)/shard_map/psum | solution.py:59
  242.1 2.6 multiply_convert_fusion.1
  244.7 42.9 %all-gather.5.cloned.1.call-done = bf16[4096,256]{1,0:T(8,128)(2,1)} async-done(((bf16[256,256]{1,0:T(8,128)(2,1)}), bf16[4096,256]{1,0:T(8,128)(2,1)}) %all-gather.5.cloned.1.call-update) | async-done | bytes 2097168 | tf_op jit(solution)/shard_map/all_gather | solution.py:62
  287.6 0.0 copy-done
  287.6 5.2 %multiply_convert_fusion = (bf16[4096,256]{1,0:T(8,128)(2,1)S(1)}, f32[4096,256]{1,0:T(8,128)}) fusion(bf16[4096,256]{1,0:T(8,128)(2,1)} %all-gather.5.cloned.1.call-done, bf16[4096,256]{1,0:T(8,128)(2,1)S(1)} %multiply_convert_fusion.1, bf16[256,256]{1,0:T(8,128)(2,1)S(1)} %copy-done), kind=kOutput, calls=%fused_computation.34 | convolution fusion | flops 547356672 | bytes 10616832 | tf_op jit(solution)/shard_map/dot_general | solution.py:61
  292.9 1.9 fusion.12
  294.8 0.9 fusion.13
  295.7 0.0 all-reduce.6.cloned.1.call-update
  295.8 0.0 reduce-scatter.2.cloned.1.call-start
  295.8 0.1 broadcast_in_dim.55
  296.0 92.9 %while.21 = (s32[]{:T(128)}, f32[16,32768]{1,0:T(8,128)S(1)}, s32[]{:T(128)}, s32[128]{0:T(128)S(1)}, s32[]{:T(128)}, /*index=5*/s32[128]{0:T(128)S(1)}, bf16[32...) while((s32[]{:T(128)}, f32[16,32768]{1,0:T(8,128)S(1)}, s32[]{:T(128)}, ...), condition=%wide.region_6.7_spmd, body=%wide.region_4.6_spmd.sunk | while | flops 1086327552 | bytes 197141120 | solution.py:37
  296.2 8.2 %gather_fusion.1 = bf16[128,128,256]{2,1,0:T(8,128)(2,1)} fusion(bf16[32,128,256]{2,1,0:T(8,128)(2,1)} %get-tuple-element.307, s32[1024]{0:T(1024)S(1)} %pad_clamp_fusion.5), kind=kCustom, calls=%fused_computation.1.clone.1 | custom fusion | bytes 16777728 | tf_op jit(solution)/shard_map/while/body/jit(_take)/gather | solution.py:22
  304.4 0.7 compare_and_fusion.5
  305.0 12.9 %convolution_bitcast_fusion.5 = f32[128,128,256]{1,2,0:T(8,128)} fusion(bf16[128,128,128]{2,1,0:T(8,128)(2,1)} %get-tuple-element.308, bf16[128,128,256]{2,1,0:T(8,128)(2,1)} %gather_fusion.1, pred[128]{0:T(512)(128)(4,1)S(1)} %get-tuple-element.249), kind=kOutput, calls=%fused_computation.19.clone.1 | convolution fusion | flops 1077936128 | bytes 29360256 | tf_op jit(solution)/shard_map/while/body/trc,trh->tch/dot_general | solution.py:24
  317.9 17.6 %copy.31 = f32[128,128,256]{0,2,1:T(8,128)} copy(f32[128,128,256]{1,2,0:T(8,128)} %convolution_bitcast_fusion.5) | data formatting | bytes 33554432 | tf_op jit(solution)/shard_map/while/body/trc,trh->tch/dot_general | solution.py:24
  335.5 11.3 %bitcast_select_fusion.5 = f32[128,32768]{0,1:T(8,128)} fusion(f32[128,128,256]{0,2,1:T(8,128)} %copy.31, pred[128]{0:T(512)(128)(4,1)S(1)} %get-tuple-element.250), kind=kLoop, calls=%fused_computation.18.clone.1 | loop fusion | flops 4194304 | bytes 33554560 | tf_op jit(solution)/shard_map/while/body/jit(_where)/select_n | solution.py:33
  346.8 17.4 %copy.32 = f32[128,32768]{1,0:T(8,128)} copy(f32[128,32768]{0,1:T(8,128)} %bitcast_select_fusion.5) | data formatting | bytes 33554432 | tf_op jit(solution)/shard_map/while/body/jit(_where)/select_n | solution.py:33
  364.3 24.3 %scatter_fusion.1 = f32[16,32768]{1,0:T(8,128)S(1)} fusion(f32[16,32768]{1,0:T(8,128)S(1)} %get-tuple-element.292, s32[128]{0:T(128)S(1)} %get-tuple-element.247, f32[128,32768]{1,0:T(8,128)} %copy.32), kind=kCustom, calls=%fused_computation.3.clone.1 | custom fusion | flops 4194304 | bytes 50332160 | tf_op jit(solution)/shard_map/while/body/scatter-add | solution.py:34
  388.8 0.0 copy-start.5
  388.8 0.0 copy-start.1
  388.8 1.5 reshape.113
  390.4 0.0 reduce-scatter.2.cloned.1.call-update
  390.4 0.0 all-reduce.8.cloned.1.call-start
  390.4 0.0 all-reduce.6.cloned.1.call-done
  390.5 0.5 all-reduce.8.cloned.1.call-update
  391.0 1.7 multiply_convert_fusion.3
  392.7 29.9 %reduce-scatter.2.cloned.1.call-done = f32[256,256]{1,0:T(8,128)} async-done(((f32[2048,256]{1,0:T(8,128)}), f32[256,256]{1,0:T(8,128)}) %reduce-scatter.2.cloned.1.call-update) | async-done | bytes 262160 | tf_op jit(solution)/shard_map/reduce_scatter | solution.py:77
  422.5 0.0 copy-done.5
  422.5 1.7 multiply_convert_fusion.2
  424.2 85.8 %all-reduce.8.cloned.1.call-done = f32[256,256]{1,0:T(8,128)} async-done(((f32[256,256]{1,0:T(8,128)}), f32[256,256]{1,0:T(8,128)}) %all-reduce.8.cloned.1.call-update) | async-done | bytes 262160 | tf_op jit(solution)/shard_map/psum | solution.py:73
  510.0 1.7 copy.52
  511.7 0.0 copy-done.1
  (5 shorter events, 0.0 us)
Async XLA Ops:
  7.2 280.5 %copy-start = (bf16[256,256]{1,0:T(8,128)(2,1)S(1)}, bf16[256,256]{1,0:T(8,128)(2,1)}, u32[]{:S(2)}) copy-start(bf16[256,256]{1,0:T(8,128)(2,1)} %param.18) | copy-start | bytes 393220
  7.2 30.3 %all-gather.3.cloned.1.call-start = ((), (), s32[]{:S(2)}) async-start(), calls=%async_computation.1 | async-start | bytes 1179648 | tf_op jit(solution)/shard_map/all_gather | solution.py:51
  8.0 0.6 copy-start.4
  10.3 231.9 %all-reduce.4.cloned.1.call-start = ((), (), s32[]{:S(2)}) async-start(), calls=%async_computation.2 | async-start | bytes 8388608 | tf_op jit(solution)/shard_map/psum | solution.py:59
  37.5 2.3 copy-start.2
  139.5 0.8 copy-start.3
  139.5 148.1 %all-gather.5.cloned.1.call-start = ((), (), s32[]{:S(2)}) async-start(), calls=%async_computation.3 | async-start | bytes 2228224 | tf_op jit(solution)/shard_map/all_gather | solution.py:62
  140.3 250.2 %all-reduce.6.cloned.1.call-start = ((), (), s32[]{:S(2)}) async-start(), calls=%async_computation.5 | async-start | bytes 524288 | tf_op jit(solution)/shard_map/psum | solution.py:73
  295.8 126.7 %reduce-scatter.2.cloned.1.call-start = ((), (), s32[]{:S(2)}) async-start(), calls=%async_computation.4 | async-start | bytes 2359296 | tf_op jit(solution)/shard_map/reduce_scatter | solution.py:77
  388.8 33.7 %copy-start.5 = (f32[256]{0:T(256)S(1)}, f32[256]{0:T(256)}, u32[]{:S(2)}) copy-start(f32[256]{0:T(256)} %copy-done.4) | copy-start | bytes 3076
  388.8 122.9 %copy-start.1 = (bf16[256,256]{1,0:T(8,128)(2,1)S(1)}, bf16[256,256]{1,0:T(8,128)(2,1)}, u32[]{:S(2)}) copy-start(bf16[256,256]{1,0:T(8,128)(2,1)} %param.18) | copy-start | bytes 393220
  390.4 119.6 %all-reduce.8.cloned.1.call-start = ((), (), s32[]{:S(2)}) async-start(), calls=%async_computation.6 | async-start | bytes 524288 | tf_op jit(solution)/shard_map/psum | solution.py:73
Sparse Core Ops, SparseCore 0:
  10.4 27.0 all-gather.2
  139.7 102.4 all-reduce.3
  244.3 43.3 all-gather.4
  295.9 59.3 all-reduce.5
  390.5 31.9 reduce-scatter.1
  425.5 84.4 all-reduce.7
